TPU v7x, 32 devices: a whole 2x2x4 slice. The times are simulated.
32 devices in a mesh: shard: 4 (over y, core), rep: 8 (over z, x).
Axes of the slice: x: 2, y: 2, z: 4, core: 2. Of those that a mesh axis runs over, the one named last changes fastest.
Arguments:
- tokens: bfloat16 [8, 512, 768], P('rep', 'shard'), may hold values from -6 to 6
- gain_one: bfloat16 [768], P('shard'), may hold values from 0.5 to 1.5
- qkv_weight: bfloat16 [768, 2304], P('shard'), may hold values from -6 to 6
- out_weight: bfloat16 [768, 768], P('shard'), may hold values from -2.5 to 2.5
- gain_two: bfloat16 [768], P('shard'), may hold values from 0.5 to 1.5
- in_weight: bfloat16 [768, 2304], P('shard'), may hold values from -0.21875 to 0.21875
- down_weight: bfloat16 [1152, 768], P('shard'), may hold values from -0.1875 to 0.1875
- grad_output: bfloat16 [8, 512, 768], P('rep', 'shard'), may hold values from -6 to 6
Outputs:
- output: bfloat16 [8, 512, 768], P('rep', 'shard')
- grad_tokens: float32 [8, 512, 768], P('rep', 'shard')
- grad_gain_one: float32 [768], P('shard')
- grad_qkv: float32 [768, 2304], P('shard')
- grad_out: float32 [768, 768], P('shard')
- grad_gain_two: float32 [768], P('shard')
- grad_in: float32 [768, 2304], P('shard')
- grad_down: float32 [1152, 768], P('shard')
All inputs are finite; a program needn't handle non-finite values.
Results may differ from a plain program's by a relative error of at most 0.02.
Values may be sent and summed in bfloat16 or wider, within the bound.
A program may use at most 128 MiB of HBM per device.

v0:
```python
import jax
import jax.numpy as jnp
from jax import lax
from jax.sharding import PartitionSpec as P

HEAD_DIM = 64
EPSILON = 1e-05
THETA = 160000.0
SQRT_HALF = 0.7071067811865476
INV_SQRT_TAU = 0.3989422804014327


def layer_norm(values, gain):
    mean_row = jnp.mean(values, axis=-1, keepdims=True)
    centred = values - mean_row
    variance = jnp.mean(centred * centred, axis=-1, keepdims=True)
    inverse = lax.rsqrt(variance + EPSILON)
    normed = centred * inverse
    return (normed, inverse, normed * gain.astype(jnp.float32))


def norm_backward(grad_out, normed, inverse, gain):
    grad_normed = grad_out * gain.astype(jnp.float32)
    gain_grad = jnp.sum(grad_out * normed, axis=0)
    first = jnp.mean(grad_normed, axis=-1, keepdims=True)
    second = jnp.mean(grad_normed * normed, axis=-1, keepdims=True)
    return (inverse * (grad_normed - first - normed * second), gain_grad)


def rotary_tables(positions, head_dim):
    half = head_dim // 2
    freq = THETA ** (-jnp.arange(half, dtype=jnp.float32) * 2.0 / head_dim)
    angles = positions.astype(jnp.float32)[:, None] * freq[None, :]
    angles = jnp.concatenate([angles, angles], axis=-1)
    return (jnp.cos(angles)[:, None, :], jnp.sin(angles)[:, None, :])


def rotate_half(values):
    half = values.shape[-1] // 2
    return jnp.concatenate([-values[..., half:], values[..., :half]], axis=-1)


def gelu_pair(inner):
    cdf = 0.5 * (1.0 + jax.scipy.special.erf(inner * SQRT_HALF))
    return (inner * cdf, cdf + inner * jnp.exp(-0.5 * inner * inner) * INV_SQRT_TAU)


def outer_sum(left, right):
    return lax.dot_general(
        left, right, (((0,), (0,)), ((), ())), preferred_element_type=jnp.float32
    )


def times_transposed(left, weight):
    return lax.dot_general(
        left, weight, (((1,), (1,)), ((), ())), preferred_element_type=jnp.float32
    )


def local(tokens, gain_one, qkv_weight, out_weight, gain_two, in_weight, down_weight, grad_output):
    tok_dev = tokens.shape[1]
    width = tokens.shape[2]
    heads = width // HEAD_DIM
    scale = HEAD_DIM ** (-0.5)
    gathered = (
        lax.all_gather(gain_one, "shard", axis=0, tiled=True),
        lax.all_gather(qkv_weight, "shard", axis=0, tiled=True),
        lax.all_gather(out_weight, "shard", axis=0, tiled=True),
        lax.all_gather(gain_two, "shard", axis=0, tiled=True),
        lax.all_gather(in_weight, "shard", axis=0, tiled=True),
        lax.all_gather(down_weight, "shard", axis=0, tiled=True),
    )
    full_g1, full_qkv, full_out, full_g2, full_in, full_down = gathered
    hidden_units = full_down.shape[0]
    inputs = tokens.reshape(tok_dev, width).astype(jnp.float32)
    normed_one, inverse_one, scaled_one = layer_norm(inputs, full_g1)
    hidden_one = scaled_one.astype(jnp.bfloat16)
    projected = jnp.dot(hidden_one, full_qkv, preferred_element_type=jnp.float32)
    positions = lax.axis_index("shard") * tok_dev + jnp.arange(tok_dev, dtype=jnp.int32)
    cosine, sine = rotary_tables(positions, HEAD_DIM)
    queries = projected[:, :width].reshape(tok_dev, heads, HEAD_DIM)
    key_raw = projected[:, width : 2 * width].reshape(tok_dev, heads, HEAD_DIM)
    query_rot = (queries * cosine + rotate_half(queries) * sine).astype(jnp.bfloat16)
    key_rot = (
        (key_raw * cosine + rotate_half(key_raw) * sine)
        .astype(jnp.bfloat16)
        .reshape(tok_dev, width)
    )
    value_rows = projected[:, 2 * width :].astype(jnp.bfloat16)
    piece = (
        lax.all_gather(key_rot, "shard", axis=0, tiled=True),
        lax.all_gather(value_rows, "shard", axis=0, tiled=True),
    )
    maxima = jnp.full((heads, tok_dev), -1e30, jnp.float32)
    count = piece[0].shape[0]
    key_heads = piece[0].reshape(count, heads, HEAD_DIM)
    value_heads = piece[1].reshape(count, heads, HEAD_DIM)
    scores = (
        jnp.einsum("qhd,khd->hqk", query_rot, key_heads, preferred_element_type=jnp.float32) * scale
    )
    new_max = jnp.maximum(maxima, jnp.max(scores, axis=-1))
    expo = jnp.exp(scores - new_max[..., None])
    totals = jnp.sum(expo, axis=-1)
    accum = jnp.einsum(
        "hqk,khd->hqd", expo.astype(jnp.bfloat16), value_heads, preferred_element_type=jnp.float32
    )
    maxima, totals, accum = (new_max, totals, accum)
    attended = (
        (accum / totals[..., None]).transpose(1, 0, 2).reshape(tok_dev, width).astype(jnp.bfloat16)
    )
    log_sum = maxima + jnp.log(totals)
    resid = inputs + jnp.dot(attended, full_out, preferred_element_type=jnp.float32)
    normed_two, inverse_two, scaled_two = layer_norm(resid, full_g2)
    hidden_two = scaled_two.astype(jnp.bfloat16)
    upper = jnp.dot(hidden_two, full_in, preferred_element_type=jnp.float32)
    inner = upper[:, :hidden_units]
    gate_half = upper[:, hidden_units:]
    gelu_value, gelu_slope = gelu_pair(inner)
    act = (gelu_value * gate_half).astype(jnp.bfloat16)
    output = (resid + jnp.dot(act, full_down, preferred_element_type=jnp.float32)).astype(
        jnp.bfloat16
    )
    regathered = (
        lax.all_gather(gain_one, "shard", axis=0, tiled=True),
        lax.all_gather(qkv_weight, "shard", axis=0, tiled=True),
        lax.all_gather(out_weight, "shard", axis=0, tiled=True),
        lax.all_gather(gain_two, "shard", axis=0, tiled=True),
        lax.all_gather(in_weight, "shard", axis=0, tiled=True),
        lax.all_gather(down_weight, "shard", axis=0, tiled=True),
    )
    full_g1, full_qkv, full_out, full_g2, full_in, full_down = regathered
    grad_b = grad_output.reshape(tok_dev, width)
    grad_f = grad_b.astype(jnp.float32)
    grad_down = outer_sum(act, grad_b)
    grad_act = times_transposed(grad_b, full_down)
    grad_upper = jnp.concatenate(
        [grad_act * gate_half * gelu_slope, grad_act * gelu_value], axis=-1
    ).astype(jnp.bfloat16)
    grad_in = outer_sum(hidden_two, grad_upper)
    grad_h2 = times_transposed(grad_upper, full_in)
    norm_grad_two, grad_gain_two = norm_backward(grad_h2, normed_two, inverse_two, full_g2)
    grad_resid = grad_f + norm_grad_two
    resid_b = grad_resid.astype(jnp.bfloat16)
    grad_out = outer_sum(attended, resid_b)
    grad_att = times_transposed(resid_b, full_out).astype(jnp.bfloat16)
    grad_heads = grad_att.reshape(tok_dev, heads, HEAD_DIM)
    att_heads = attended.reshape(tok_dev, heads, HEAD_DIM)
    delta = jnp.sum(grad_heads.astype(jnp.float32) * att_heads.astype(jnp.float32), axis=-1).T
    piece = (
        lax.all_gather(key_rot, "shard", axis=0, tiled=True),
        lax.all_gather(value_rows, "shard", axis=0, tiled=True),
    )
    count = piece[0].shape[0]
    key_heads = piece[0].reshape(count, heads, HEAD_DIM)
    value_heads = piece[1].reshape(count, heads, HEAD_DIM)
    scores = (
        jnp.einsum("qhd,khd->hqk", query_rot, key_heads, preferred_element_type=jnp.float32) * scale
    )
    probs = jnp.exp(scores - log_sum[..., None])
    value_piece = jnp.einsum(
        "hqk,qhd->khd", probs.astype(jnp.bfloat16), grad_heads, preferred_element_type=jnp.float32
    )
    grad_probs = jnp.einsum(
        "qhd,khd->hqk", grad_heads, value_heads, preferred_element_type=jnp.float32
    )
    grad_scores = (probs * (grad_probs - delta[..., None]) * scale).astype(jnp.bfloat16)
    grad_query = jnp.einsum(
        "hqk,khd->qhd", grad_scores, key_heads, preferred_element_type=jnp.float32
    )
    key_piece = jnp.einsum(
        "hqk,qhd->khd", grad_scores, query_rot, preferred_element_type=jnp.float32
    )
    key_total = key_piece.reshape(count, width)
    value_total = value_piece.reshape(count, width)
    grad_qr, key_total, value_total = (grad_query, key_total, value_total)
    grad_kr, grad_value = (
        lax.psum_scatter(
            key_total.astype(jnp.bfloat16), "shard", scatter_dimension=0, tiled=True
        ).astype(jnp.float32),
        lax.psum_scatter(
            value_total.astype(jnp.bfloat16), "shard", scatter_dimension=0, tiled=True
        ).astype(jnp.float32),
    )
    grad_kr = grad_kr.reshape(tok_dev, heads, HEAD_DIM)
    grad_q = grad_qr * cosine - rotate_half(grad_qr) * sine
    grad_k = grad_kr * cosine - rotate_half(grad_kr) * sine
    grad_projected = jnp.concatenate(
        [grad_q.reshape(tok_dev, width), grad_k.reshape(tok_dev, width), grad_value], axis=-1
    ).astype(jnp.bfloat16)
    grad_qkv = outer_sum(hidden_one, grad_projected)
    grad_h1 = times_transposed(grad_projected, full_qkv)
    norm_grad_one, grad_gain_one = norm_backward(grad_h1, normed_one, inverse_one, full_g1)
    grad_tokens = grad_resid + norm_grad_one
    owned = (
        lax.psum_scatter(
            grad_gain_one.astype(jnp.bfloat16), "shard", scatter_dimension=0, tiled=True
        ).astype(jnp.float32),
        lax.psum_scatter(
            grad_qkv.astype(jnp.bfloat16), "shard", scatter_dimension=0, tiled=True
        ).astype(jnp.float32),
        lax.psum_scatter(
            grad_out.astype(jnp.bfloat16), "shard", scatter_dimension=0, tiled=True
        ).astype(jnp.float32),
        lax.psum_scatter(
            grad_gain_two.astype(jnp.bfloat16), "shard", scatter_dimension=0, tiled=True
        ).astype(jnp.float32),
        lax.psum_scatter(
            grad_in.astype(jnp.bfloat16), "shard", scatter_dimension=0, tiled=True
        ).astype(jnp.float32),
        lax.psum_scatter(
            grad_down.astype(jnp.bfloat16), "shard", scatter_dimension=0, tiled=True
        ).astype(jnp.float32),
    )
    summed = lax.psum((owned[0], owned[1], owned[2], owned[3], owned[4], owned[5]), "rep")
    return (
        output.reshape(1, tok_dev, width),
        grad_tokens.reshape(1, tok_dev, width),
        summed[0],
        summed[1],
        summed[2],
        summed[3],
        summed[4],
        summed[5],
    )


def solution(mesh):
    in_specs = (
        P("rep", "shard", None),
        P("shard"),
        P("shard", None),
        P("shard", None),
        P("shard"),
        P("shard", None),
        P("shard", None),
        P("rep", "shard", None),
    )
    out_specs = (
        P("rep", "shard", None),
        P("rep", "shard", None),
        P("shard"),
        P("shard", None),
        P("shard", None),
        P("shard"),
        P("shard", None),
        P("shard", None),
    )
    return jax.shard_map(local, mesh=mesh, in_specs=in_specs, out_specs=out_specs, check_vma=False)
```

profile of v0, /device:TPU:0, one launch (start us, length us, event | category | flops | bytes accessed | tf_op | source)
XLA Modules:
  0.0 537.6 jit_solution(9330633500089407364)
XLA Ops:
  7.3 0.7 all-gather.5.cloned.1.call-update
  8.0 0.7 all-gather.7.cloned.1.call-update
  8.7 0.7 all-gather.9.cloned.1.call-update
  9.5 0.5 all-gather.11.cloned.1.call-update
  10.2 0.2 fusion.45
  10.5 0.6 fusion.70
  11.7 0.2 dynamic-update-slice
  12.0 0.2 dynamic-update-slice.1
  12.2 8.4 %all-reduce.6 = (bf16[768]{0:T(1024)(128)(2,1)S(1)}, bf16[768]{0:T(1024)(128)(2,1)S(1)}) all-reduce(bf16[768]{0:T(1024)(128)(2,1)S(1)} %dynamic-update-slice, bf16[768]{0:T(1024)(128)(2,1)S(1)} %dynamic-update-slice.1), channel_id=1, replica_groups=mesh['shard'=4,'rep'=8] {'shard'}, use_global_device_ids=true, to_apply=%add | all-reduce | flops 1536 | bytes 6144
  21.0 22.1 %all-gather.5.cloned.1.call-done = bf16[768,2304]{1,0:T(8,128)(2,1)} async-done(((bf16[192,2304]{1,0:T(8,128)(2,1)}), bf16[768,2304]{1,0:T(8,128)(2,1)}) %all-gather.5.cloned.1.call-update) | async-done | bytes 3538960 | tf_op jit(solution)/shard_map/all_gather | solution.py:67
  43.1 2.7 fusion.67
  46.4 0.2 copy.41
  46.6 8.6 %all_gather.34 = bf16[512,768]{1,0:T(8,128)(2,1)S(1)} all-gather(bf16[128,768]{1,0:T(8,128)(2,1)S(1)} %get-tuple-element.27), channel_id=1, replica_groups=mesh['shard'=4,'rep'=8] {'shard'}, dimensions={0}, use_global_device_ids=true | all-gather | bytes 983040 | tf_op jit(solution)/shard_map/all_gather | solution.py:91
  55.2 10.6 %all_gather.35 = bf16[512,768]{1,0:T(8,128)(2,1)S(1)} all-gather(bf16[128,768]{1,0:T(8,128)(2,1)S(1)} %slice.87), channel_id=1, replica_groups=mesh['shard'=4,'rep'=8] {'shard'}, dimensions={0}, use_global_device_ids=true | all-gather | bytes 983040 | tf_op jit(solution)/shard_map/all_gather | solution.py:92
  65.7 0.7 fusion.47
  66.5 1.3 copy.45
  67.7 1.2 copy.46
  68.9 1.8 multiply_reduce_fusion
  70.8 0.9 fusion
  71.6 0.3 copy-done.9
  71.9 1.5 fusion.20
  73.5 2.2 fusion.71
  75.7 0.2 multiply_reduce_fusion.4
  75.9 0.4 copy-done.37
  76.3 0.5 add_rsqrt_fusion
  76.9 19.5 %all-gather.9.cloned.1.call-done = bf16[768,2304]{1,0:T(8,128)(2,1)} async-done(((bf16[192,2304]{1,0:T(8,128)(2,1)}), bf16[768,2304]{1,0:T(8,128)(2,1)}) %all-gather.9.cloned.1.call-update) | async-done | bytes 3538960 | tf_op jit(solution)/shard_map/all_gather | solution.py:70
  96.4 3.7 fusion.69
  100.1 18.5 %all-gather.11.cloned.1.call-done = bf16[1152,768]{1,0:T(8,128)(2,1)} async-done(((bf16[288,768]{1,0:T(8,128)(2,1)}), bf16[1152,768]{1,0:T(8,128)(2,1)}) %all-gather.11.cloned.1.call-update) | async-done | bytes 1769488 | tf_op jit(solution)/shard_map/all_gather | solution.py:71
  118.6 3.4 fusion.30
  122.0 1.9 multiply_reduce_fusion.1
  123.9 0.2 multiply_add_fusion
  124.1 0.7 copy-done.5
  124.8 1.2 convolution_convert_fusion.5
  126.1 1.8 copy.47
  127.8 1.1 multiply_reduce_fusion.2
  128.9 2.3 multiply_convert_fusion
  131.3 1.1 copy-done
  132.4 1.2 convolution_convert_fusion.4
  133.7 2.3 copy.48
  136.0 2.6 fusion.11
  138.7 2.4 copy.50
  141.1 0.2 reduce-scatter.13.cloned.1.call-start
  141.3 1.5 convolution_convert_fusion.3
  143.0 1.9 convolution_convert_fusion.2
  144.9 3.0 convolution_convert_fusion
  148.0 1.3 copy-done.1
  149.3 0.2 copy-done.4
  149.5 0.6 convolution_bitcast_fusion
  150.3 9.1 %reduce-scatter.19.cloned.1.call-done = bf16[128,768]{1,0:T(8,128)(2,1)} async-done(((bf16[512,768]{1,0:T(8,128)(2,1)}), bf16[128,768]{1,0:T(8,128)(2,1)}) %reduce-scatter.19.cloned.1.call-update) | async-done | bytes 196624
  159.4 1.1 copy.49
  160.5 0.9 fusion.49
  161.5 23.5 %reduce-scatter.21.cloned.1.call-done = bf16[128,768]{1,0:T(8,128)(2,1)} async-done(((bf16[512,768]{1,0:T(8,128)(2,1)}), bf16[128,768]{1,0:T(8,128)(2,1)}) %reduce-scatter.21.cloned.1.call-update) | async-done | bytes 196624
  185.0 1.1 copy.51
  186.1 3.1 convolution_convert_fusion.1
  190.1 0.7 copy-done.13
  190.7 1.1 fusion.24
  191.9 3.6 fusion.44
  195.5 5.8 %all-reduce.5 = (bf16[768]{0:T(1024)(128)(2,1)S(1)}, bf16[768]{0:T(1024)(128)(2,1)S(1)}) all-reduce(bf16[768]{0:T(1024)(128)(2,1)S(1)} %get-tuple-element.10, bf16[768]{0:T(1024)(128)(2,1)S(1)} %copy-done.43), channel_id=4, replica_groups=mesh['shard'=4,'rep'=8] {'shard'}, use_global_device_ids=true, to_apply=%region_14.0.clone | all-reduce | flops 1536 | bytes 6144
  201.4 0.9 fusion.43
  202.3 10.9 %reduce-scatter.13.cloned.1.call-done = bf16[192,768]{1,0:T(8,128)(2,1)} async-done(((bf16[768,768]{1,0:T(8,128)(2,1)}), bf16[192,768]{1,0:T(8,128)(2,1)}) %reduce-scatter.13.cloned.1.call-update) | async-done | bytes 294928 | tf_op jit(solution)/shard_map/reduce_scatter | solution.py:201
  213.2 32.4 %reduce-scatter.17.cloned.1.call-done = bf16[288,768]{1,0:T(8,128)(2,1)} async-done(((bf16[1152,768]{1,0:T(8,128)(2,1)}), bf16[288,768]{1,0:T(8,128)(2,1)}) %reduce-scatter.17.cloned.1.call-update) | async-done | bytes 442384 | tf_op jit(solution)/shard_map/reduce_scatter | solution.py:210
  245.6 43.0 %reduce-scatter.15.cloned.1.call-done = bf16[192,2304]{1,0:T(8,128)(2,1)} async-done(((bf16[768,2304]{1,0:T(8,128)(2,1)}), bf16[192,2304]{1,0:T(8,128)(2,1)}) %reduce-scatter.15.cloned.1.call-update) | async-done | bytes 884752 | tf_op jit(solution)/shard_map/reduce_scatter | solution.py:207
  288.5 42.8 %reduce-scatter.11.cloned.1.call-done = bf16[192,2304]{1,0:T(8,128)(2,1)} async-done(((bf16[768,2304]{1,0:T(8,128)(2,1)}), bf16[192,2304]{1,0:T(8,128)(2,1)}) %reduce-scatter.11.cloned.1.call-update) | async-done | bytes 884752 | tf_op jit(solution)/shard_map/reduce_scatter | solution.py:198
  331.3 199.4 %all-reduce.8 = (f32[192]{0:T(256)}, f32[192,2304]{1,0:T(8,128)}, f32[192,768]{1,0:T(8,128)}, f32[192]{0:T(256)}, f32[192,2304]{1,0:T(8,128)}, /*index=5*/f32[288,768]{1,0:T(8,128)}) all-reduce(f32[192]{0:T(256)S(1)} %dynamic-slice_convert_fusion.1, ...), channel_id=1, replica_groups=mesh['shard'=4,'rep'=8] {'rep'}, use_global_device_ids=true, to_apply=%region_15.0 | all-reduce | flops 1253760 | bytes 7523328 | tf_op jit(solution)/shard_map/psum | solution.py:214
  (135 shorter events, 2.0 us)
Async XLA Ops:
  7.2 3.3 copy-start.42
  7.2 2.9 copy-start.2
  7.2 4.5 copy-start.44
  7.2 4.8 copy-start.45
  7.2 35.9 %all-gather.5.cloned.1.call-start = ((), (), s32[]{:S(2)}) async-start(), calls=%async_computation.6 | async-start | bytes 4423680 | tf_op jit(solution)/shard_map/all_gather | solution.py:67
  7.9 65.5 %all-gather.7.cloned.1.call-start = ((), (), s32[]{:S(2)}) async-start(), calls=%async_computation.7 | async-start | bytes 1474560 | tf_op jit(solution)/shard_map/all_gather | solution.py:68
  8.7 87.7 %all-gather.9.cloned.1.call-start = ((), (), s32[]{:S(2)}) async-start(), calls=%async_computation.8 | async-start | bytes 4423680 | tf_op jit(solution)/shard_map/all_gather | solution.py:70
  9.4 109.2 %all-gather.11.cloned.1.call-start = ((), (), s32[]{:S(2)}) async-start(), calls=%async_computation.9 | async-start | bytes 2211840 | tf_op jit(solution)/shard_map/all_gather | solution.py:71
  10.0 149.3 %reduce-scatter.19.cloned.1.call-start = ((), (), s32[]{:S(2)}) async-start(), calls=%async_computation.14 | async-start | bytes 983040
  10.2 35.5 %copy-start.33 = (f32[128]{0:T(128)}, f32[128]{0:T(128)S(1)}, u32[]{:S(2)}) copy-start(f32[128]{0:T(128)S(1)} %broadcast_multiply_fusion.6) | copy-start | bytes 1540
  10.5 35.3 %copy-start.35 = (f32[128]{0:T(128)}, f32[128]{0:T(128)S(1)}, u32[]{:S(2)}) copy-start(f32[128]{0:T(128)S(1)} %add_rsqrt_fusion.1) | copy-start | bytes 1540
  20.8 45.0 %copy-start.16 = (f32[128,64]{0,1:T(8,128)}, f32[128,64]{0,1:T(8,128)S(1)}, u32[]{:S(2)}) copy-start(f32[128,64]{0,1:T(8,128)S(1)} %get-tuple-element.37) | copy-start | bytes 98308
  20.8 45.0 %copy-start.24 = (f32[128,64]{0,1:T(8,128)}, f32[128,64]{0,1:T(8,128)S(1)}, u32[]{:S(2)}) copy-start(f32[128,64]{0,1:T(8,128)S(1)} %get-tuple-element.38) | copy-start | bytes 98308
  66.5 2.4 copy-start.10
  70.7 2.7 copy-start.29
  70.7 1.2 copy-start.9
  71.6 1.8 copy-start.31
  73.5 3.4 copy-start.30
  73.5 3.4 copy-start.32
  75.7 0.6 copy-start.37
  118.6 3.4 copy-start.8
  118.6 3.4 copy-start.38
  118.6 3.4 copy-start.40
  122.0 1.9 copy-start.25
  122.0 1.9 copy-start.27
  122.0 1.9 copy-start.22
  122.0 2.8 copy-start.7
  124.1 0.7 copy-start.5
  128.9 3.5 copy-start.11
  131.3 1.1 copy-start
  136.0 49.0 %reduce-scatter.21.cloned.1.call-start = ((), (), s32[]{:S(2)}) async-start(), calls=%async_computation.15 | async-start | bytes 983040
  138.6 2.7 copy-start.6
  138.6 2.7 copy-start.12
  138.6 4.3 copy-start.14
  138.6 4.3 copy-start.23
  141.1 72.1 %reduce-scatter.13.cloned.1.call-start = ((), (), s32[]{:S(2)}) async-start(), calls=%async_computation.11 | async-start | bytes 1474560 | tf_op jit(solution)/shard_map/reduce_scatter | solution.py:201
  142.9 2.0 copy-start.26
  142.9 2.1 copy-start.28
  142.9 2.1 copy-start.39
  142.9 2.1 copy-start.41
  142.9 102.7 %reduce-scatter.17.cloned.1.call-start = ((), (), s32[]{:S(2)}) async-start(), calls=%async_computation.13 | async-start | bytes 2211840 | tf_op jit(solution)/shard_map/reduce_scatter | solution.py:210
  144.9 143.7 %reduce-scatter.15.cloned.1.call-start = ((), (), s32[]{:S(2)}) async-start(), calls=%async_computation.12 | async-start | bytes 4423680 | tf_op jit(solution)/shard_map/reduce_scatter | solution.py:207
  147.9 1.4 copy-start.1
  147.9 1.6 copy-start.4
  147.9 183.4 %reduce-scatter.11.cloned.1.call-start = ((), (), s32[]{:S(2)}) async-start(), calls=%async_computation.10 | async-start | bytes 4423680 | tf_op jit(solution)/shard_map/reduce_scatter | solution.py:198
  150.2 11.2 %copy-start.17 = (f32[128,64]{0,1:T(8,128)S(1)}, f32[128,64]{0,1:T(8,128)}, u32[]{:S(2)}) copy-start(f32[128,64]{0,1:T(8,128)} %copy-done.16) | copy-start | bytes 98308
  150.2 35.9 %copy-start.3 = (bf16[1,128,768]{2,1,0:T(8,128)(2,1)S(1)}, bf16[1,128,768]{2,1,0:T(8,128)(2,1)}, u32[]{:S(2)}) copy-start(bf16[1,128,768]{2,1,0:T(8,128)(2,1)} %param.8) | copy-start | bytes 589828
  150.2 35.9 %copy-start.34 = (f32[128]{0:T(128)S(1)}, f32[128]{0:T(128)}, u32[]{:S(2)}) copy-start(f32[128]{0:T(128)} %copy-done.33) | copy-start | bytes 1540
  150.2 35.9 %copy-start.36 = (f32[128]{0:T(128)S(1)}, f32[128]{0:T(128)}, u32[]{:S(2)}) copy-start(f32[128]{0:T(128)} %copy-done.35) | copy-start | bytes 1540
  161.4 24.7 %copy-start.18 = (bf16[128,12,64]{0,2,1:T(8,128)(2,1)}, bf16[128,12,64]{0,2,1:T(8,128)(2,1)S(1)}, u32[]{:S(2)}) copy-start(bf16[128,12,64]{0,2,1:T(8,128)(2,1)S(1)} %get-tuple-element.35) | copy-start | bytes 589828
  161.5 24.6 %copy-start.20 = (bf16[128,768]{0,1:T(8,128)(2,1)}, bf16[128,768]{0,1:T(8,128)(2,1)S(1)}, u32[]{:S(2)}) copy-start(bf16[128,768]{0,1:T(8,128)(2,1)S(1)} %fusion.50) | copy-start | bytes 589828
  189.2 1.5 copy-start.13
  189.2 1.5 copy-start.15
  189.2 2.6 copy-start.19
  190.7 1.1 copy-start.21
  191.9 3.6 copy-start.43
Sparse Core Ops, SparseCore 0:
  9.6 33.4 all-gather.4
  44.6 19.3 all-gather.6
  65.6 30.7 all-gather.8
  97.8 20.7 all-gather.10
  136.1 23.2 reduce-scatter.18
  161.7 23.2 reduce-scatter.20
  187.6 25.5 reduce-scatter.12
  216.3 29.1 reduce-scatter.16
  248.1 40.3 reduce-scatter.14
  290.9 40.3 reduce-scatter.10
where the time goes:
time: 538 us
  blocking collectives  233 us (43%)
  waiting for transfers between devices  224 us (42%)
  matrix products  39.5 us (7%)
  local copies, waits for them, and re-layouts  17.8 us (3%)
  between operations  16.3 us (3%)
  other arithmetic  6.33 us (1%)
    psum x1, blocking collectives, local(): lax.psum((owned[0], owned[1], owned[2], owned[3], owned[4], owned[5]), 'r...  199 us
    reduce_scatter x1, waiting for transfers between devices, local(): lax.psum_scatter(grad_in.astype(jnp.bfloat16), 'shard', scatter_dimension...  43 us
    reduce_scatter x1, waiting for transfers between devices, local(): lax.psum_scatter(grad_qkv.astype(jnp.bfloat16), 'shard', scatter_dimensio...  42.8 us
    unnamed x12, waiting for transfers between devices  35.3 us
    reduce_scatter x1, waiting for transfers between devices, local(): lax.psum_scatter(grad_down.astype(jnp.bfloat16), 'shard', scatter_dimensi...  32.4 us
    all_gather x1, waiting for transfers between devices, local(): lax.all_gather(qkv_weight, 'shard', axis=0, tiled=True)  22.1 us
    all_gather x1, waiting for transfers between devices, local(): lax.all_gather(in_weight, 'shard', axis=0, tiled=True)  19.5 us
    all_gather x1, waiting for transfers between devices, local(): lax.all_gather(down_weight, 'shard', axis=0, tiled=True)  18.5 us
  transfers between devices with their start and end apart: 10, of which 9 were waited for; matrix products, arithmetic and copies ran while one was open for 8% of the time, Pallas kernels for 0%

commit v1 on v0

--- a/solution.py
+++ b/solution.py
@@ -67,7 +67,9 @@
         lax.all_gather(qkv_weight, "shard", axis=0, tiled=True),
         lax.all_gather(out_weight, "shard", axis=0, tiled=True),
         lax.all_gather(gain_two, "shard", axis=0, tiled=True),
-        lax.all_gather(in_weight, "shard", axis=0, tiled=True),
+        jnp.concatenate(
+            lax.all_to_all(jnp.stack([in_weight] * lax.axis_size("shard")), "shard", 0, 0), axis=0
+        ),
         lax.all_gather(down_weight, "shard", axis=0, tiled=True),
     )
     full_g1, full_qkv, full_out, full_g2, full_in, full_down = gathered

time: 538 us -> 564 us (1.048)
  blocking collectives: 233 us -> 293 us
  waiting for transfers between devices: 224 us -> 179 us
    unnamed x2, blocking collectives: 14.1 us -> 69.2 us
    all_gather x1, waiting for transfers between devices: 22.1 us -> 0.02 us  [local(): lax.all_gather(qkv_weight, 'shard', axis=0, tiled=True)]
    all_gather x1, waiting for transfers between devices: 18.5 us -> 0.01 us  [local(): lax.all_gather(down_weight, 'shard', axis=0, tiled=True)]
    unnamed x101 -> x79, local copies, waits for them, and re-layouts: 12.9 us -> 12.3 us
  transfers between devices with their start and end apart: 10 -> 11, of which waited for: 9 -> 7; matrix products, arithmetic and copies ran while one was open for 8% -> 9% of each run, Pallas kernels for 0% -> 0%
where the time goes in v1:
time: 564 us
  blocking collectives  293 us (52%)
  waiting for transfers between devices  179 us (32%)
  matrix products  44.1 us (8%)
  local copies, waits for them, and re-layouts  20.3 us (4%)
  between operations  16.2 us (3%)
  other arithmetic  5.65 us (1%)
    psum x1, blocking collectives, local(): lax.psum((owned[0], owned[1], owned[2], owned[3], owned[4], owned[5]), 'r...  199 us
    unnamed x2, blocking collectives  69.2 us
    reduce_scatter x1, waiting for transfers between devices, local(): lax.psum_scatter(grad_in.astype(jnp.bfloat16), 'shard', scatter_dimension...  43 us
    reduce_scatter x1, waiting for transfers between devices, local(): lax.psum_scatter(grad_qkv.astype(jnp.bfloat16), 'shard', scatter_dimensio...  42.8 us
    unnamed x12, waiting for transfers between devices  35.3 us
    reduce_scatter x1, waiting for transfers between devices, local(): lax.psum_scatter(grad_down.astype(jnp.bfloat16), 'shard', scatter_dimensi...  32.3 us
    all_gather x1, waiting for transfers between devices, local(): lax.all_gather(in_weight, 'shard', axis=0, tiled=True)  14.9 us
    all_gather x1, blocking collectives, local(): lax.all_gather(key_rot, 'shard', axis=0, tiled=True)  13.4 us
  transfers between devices with their start and end apart: 11, of which 7 were waited for; matrix products, arithmetic and copies ran while one was open for 9% of the time, Pallas kernels for 0%

profile of v1, /device:TPU:0, one launch (start us, length us, event | category | flops | bytes accessed | tf_op | source)
XLA Modules:
  0.0 563.6 jit_solution(12549336331367387778)
XLA Ops:
  7.2 0.7 all-gather.5.cloned.1.call-update
  7.9 0.7 all-gather.7.cloned.1.call-update
  8.7 0.7 all-gather.9.cloned.1.call-update
  9.4 3.3 stack.2
  12.7 4.9 all-to-all-start
  17.6 0.5 all-gather.11.cloned.1.call-update
  18.3 0.2 fusion.45
  18.7 0.6 fusion.70
  20.0 0.2 dynamic-update-slice
  20.2 0.2 dynamic-update-slice.1
  20.5 63.5 %all-reduce.6 = (bf16[768]{0:T(1024)(128)(2,1)S(1)}, bf16[768]{0:T(1024)(128)(2,1)S(1)}) all-reduce(bf16[768]{0:T(1024)(128)(2,1)S(1)} %dynamic-update-slice, bf16[768]{0:T(1024)(128)(2,1)S(1)} %dynamic-update-slice.1), channel_id=1, replica_groups=mesh['shard'=4,'rep'=8] {'shard'}, use_global_device_ids=true, to_apply=%add | all-reduce | flops 1536 | bytes 6144
  84.0 0.2 copy.42
  84.2 2.7 fusion.67
  87.0 10.6 %all_gather.34 = bf16[512,768]{1,0:T(8,128)(2,1)S(1)} all-gather(bf16[128,768]{1,0:T(8,128)(2,1)S(1)} %slice.87), channel_id=1, replica_groups=mesh['shard'=4,'rep'=8] {'shard'}, dimensions={0}, use_global_device_ids=true | all-gather | bytes 983040 | tf_op jit(solution)/shard_map/all_gather | solution.py:94
  97.6 1.2 copy.46
  99.0 0.2 copy.44
  99.2 0.2 copy.41
  99.4 13.4 %all_gather.33 = bf16[512,768]{1,0:T(8,128)(2,1)S(1)} all-gather(bf16[128,768]{1,0:T(8,128)(2,1)S(1)} %get-tuple-element.27), channel_id=1, replica_groups=mesh['shard'=4,'rep'=8] {'shard'}, dimensions={0}, use_global_device_ids=true | all-gather | bytes 983040 | tf_op jit(solution)/shard_map/all_gather | solution.py:93
  112.8 1.2 copy.45
  114.1 0.7 copy-done.9
  114.7 1.9 multiply_reduce_fusion
  116.7 0.6 copy-done.20
  117.3 0.9 fusion
  118.1 1.5 fusion.20
  119.7 1.9 fusion.71
  121.6 0.2 multiply_reduce_fusion.4
  121.8 0.4 copy-done.26
  122.2 0.5 add_rsqrt_fusion
  122.7 0.7 log_add_fusion
  123.4 3.8 fusion.69
  127.3 3.5 fusion.30
  130.7 14.9 %all-gather.11.cloned.1.call-done = bf16[768,2304]{1,0:T(8,128)(2,1)} async-done(((bf16[192,2304]{1,0:T(8,128)(2,1)}), bf16[768,2304]{1,0:T(8,128)(2,1)}) %all-gather.11.cloned.1.call-update) | async-done | bytes 3538960 | tf_op jit(solution)/shard_map/all_gather | solution.py:130
  145.6 4.3 multiply_reduce_fusion.1
  149.9 0.2 multiply_add_fusion
  150.1 0.7 copy-done.5
  150.9 1.2 convolution_convert_fusion.5
  152.1 1.7 copy.47
  153.8 1.1 multiply_reduce_fusion.2
  155.0 2.3 multiply_convert_fusion
  157.3 1.1 copy-done
  158.4 1.2 convolution_convert_fusion.4
  159.7 2.3 copy.48
  162.0 0.2 reduce-scatter.21.cloned.1.call-start
  162.3 2.6 fusion.11
  164.9 2.4 copy.50
  167.4 2.6 convolution_convert_fusion.3
  170.1 1.9 convolution_convert_fusion.2
  172.0 4.1 convolution_convert_fusion
  176.3 0.6 convolution_bitcast_fusion
  177.0 8.4 %reduce-scatter.19.cloned.1.call-done = bf16[128,768]{1,0:T(8,128)(2,1)} async-done(((bf16[512,768]{1,0:T(8,128)(2,1)}), bf16[128,768]{1,0:T(8,128)(2,1)}) %reduce-scatter.19.cloned.1.call-update) | async-done | bytes 196624
  185.4 1.1 copy.49
  186.7 24.3 %reduce-scatter.21.cloned.1.call-done = bf16[128,768]{1,0:T(8,128)(2,1)} async-done(((bf16[512,768]{1,0:T(8,128)(2,1)}), bf16[128,768]{1,0:T(8,128)(2,1)}) %reduce-scatter.21.cloned.1.call-update) | async-done | bytes 196624
  211.0 1.1 copy.51
  212.1 3.1 convolution_convert_fusion.1
  216.0 0.7 copy-done.11
  216.7 1.1 fusion.24
  217.8 3.6 fusion.44
  221.5 5.8 %all-reduce.5 = (bf16[768]{0:T(1024)(128)(2,1)S(1)}, bf16[768]{0:T(1024)(128)(2,1)S(1)}) all-reduce(bf16[768]{0:T(1024)(128)(2,1)S(1)} %get-tuple-element.10, bf16[768]{0:T(1024)(128)(2,1)S(1)} %copy-done.32), channel_id=4, replica_groups=mesh['shard'=4,'rep'=8] {'shard'}, use_global_device_ids=true, to_apply=%region_14.0.clone | all-reduce | flops 1536 | bytes 6144
  227.4 0.9 fusion.43
  228.4 10.9 %reduce-scatter.13.cloned.1.call-done = bf16[192,768]{1,0:T(8,128)(2,1)} async-done(((bf16[768,768]{1,0:T(8,128)(2,1)}), bf16[192,768]{1,0:T(8,128)(2,1)}) %reduce-scatter.13.cloned.1.call-update) | async-done | bytes 294928 | tf_op jit(solution)/shard_map/reduce_scatter | solution.py:203
  239.2 32.3 %reduce-scatter.17.cloned.1.call-done = bf16[288,768]{1,0:T(8,128)(2,1)} async-done(((bf16[1152,768]{1,0:T(8,128)(2,1)}), bf16[288,768]{1,0:T(8,128)(2,1)}) %reduce-scatter.17.cloned.1.call-update) | async-done | bytes 442384 | tf_op jit(solution)/shard_map/reduce_scatter | solution.py:212
  271.6 43.0 %reduce-scatter.15.cloned.1.call-done = bf16[192,2304]{1,0:T(8,128)(2,1)} async-done(((bf16[768,2304]{1,0:T(8,128)(2,1)}), bf16[192,2304]{1,0:T(8,128)(2,1)}) %reduce-scatter.15.cloned.1.call-update) | async-done | bytes 884752 | tf_op jit(solution)/shard_map/reduce_scatter | solution.py:209
  314.5 42.8 %reduce-scatter.11.cloned.1.call-done = bf16[192,2304]{1,0:T(8,128)(2,1)} async-done(((bf16[768,2304]{1,0:T(8,128)(2,1)}), bf16[192,2304]{1,0:T(8,128)(2,1)}) %reduce-scatter.11.cloned.1.call-update) | async-done | bytes 884752 | tf_op jit(solution)/shard_map/reduce_scatter | solution.py:200
  357.3 199.5 %all-reduce.8 = (f32[192]{0:T(256)}, f32[192,2304]{1,0:T(8,128)}, f32[192,768]{1,0:T(8,128)}, f32[192]{0:T(256)}, f32[192,2304]{1,0:T(8,128)}, /*index=5*/f32[288,768]{1,0:T(8,128)}) all-reduce(f32[192]{0:T(256)S(1)} %dynamic-slice_convert_fusion.1, ...), channel_id=1, replica_groups=mesh['shard'=4,'rep'=8] {'rep'}, use_global_device_ids=true, to_apply=%region_15.0 | all-reduce | flops 1253760 | bytes 7523328 | tf_op jit(solution)/shard_map/psum | solution.py:216
  (116 shorter events, 1.8 us)
Async XLA Ops:
  7.2 77.0 %all-gather.5.cloned.1.call-start = ((), (), s32[]{:S(2)}) async-start(), calls=%async_computation.7 | async-start | bytes 4423680 | tf_op jit(solution)/shard_map/all_gather | solution.py:67
  7.9 111.8 %all-gather.7.cloned.1.call-start = ((), (), s32[]{:S(2)}) async-start(), calls=%async_computation.8 | async-start | bytes 1474560 | tf_op jit(solution)/shard_map/all_gather | solution.py:68
  8.7 118.6 %all-gather.9.cloned.1.call-start = ((), (), s32[]{:S(2)}) async-start(), calls=%async_computation.9 | async-start | bytes 2211840 | tf_op jit(solution)/shard_map/all_gather | solution.py:73
  12.7 5.5 copy-start.2
  12.7 6.1 %copy-start.31 = (u32[32]{0:T(128)S(1)}, u32[32]{0:T(128)}, u32[]{:S(2)}) copy-start(u32[32]{0:T(128)} %constant.48) | copy-start | bytes 388
  12.7 7.3 %copy-start.33 = (bf16[192]{0:T(256)(128)(2,1)S(1)}, bf16[192]{0:T(256)(128)(2,1)}, u32[]{:S(2)}) copy-start(bf16[192]{0:T(256)(128)(2,1)} %param.9) | copy-start | bytes 1156
  12.7 7.6 %copy-start.34 = (bf16[192]{0:T(256)(128)(2,1)S(1)}, bf16[192]{0:T(256)(128)(2,1)}, u32[]{:S(2)}) copy-start(bf16[192]{0:T(256)(128)(2,1)} %param.12) | copy-start | bytes 1156
  12.7 110.8 %all-to-all-start = ((bf16[4,192,2304]{2,1,0:T(8,128)(2,1)}), bf16[4,192,2304]{2,1,0:T(8,128)(2,1)}, u32[]{:S(2)}, u32[]{:S(2)}) async-start(bf16[4,192,2304]{2,1,0:T(8,128)(2,1)} %stack.2), calls=%async_computation | async-start | bytes 7077888 | tf_op jit(solution)/shard_map/all_to_all | solution.py:71
  17.5 128.1 %all-gather.11.cloned.1.call-start = ((), (), s32[]{:S(2)}) async-start(), calls=%async_computation.10 | async-start | bytes 4423680 | tf_op jit(solution)/shard_map/all_gather | solution.py:130
  18.1 167.3 %reduce-scatter.19.cloned.1.call-start = ((), (), s32[]{:S(2)}) async-start(), calls=%async_computation.15 | async-start | bytes 983040
  18.3 68.6 %copy-start.22 = (f32[128]{0:T(128)}, f32[128]{0:T(128)S(1)}, u32[]{:S(2)}) copy-start(f32[128]{0:T(128)S(1)} %broadcast_multiply_fusion.6) | copy-start | bytes 1540
  18.7 95.3 %copy-start.13 = (f32[128,64]{0,1:T(8,128)}, f32[128,64]{0,1:T(8,128)S(1)}, u32[]{:S(2)}) copy-start(f32[128,64]{0,1:T(8,128)S(1)} %get-tuple-element.37) | copy-start | bytes 98308
  18.7 95.3 %copy-start.17 = (f32[128,64]{0,1:T(8,128)}, f32[128,64]{0,1:T(8,128)S(1)}, u32[]{:S(2)}) copy-start(f32[128,64]{0,1:T(8,128)S(1)} %get-tuple-element.38) | copy-start | bytes 98308
  84.2 13.4 %copy-start.24 = (f32[128]{0:T(128)}, f32[128]{0:T(128)S(1)}, u32[]{:S(2)}) copy-start(f32[128]{0:T(128)S(1)} %add_rsqrt_fusion.1) | copy-start | bytes 1540
  114.1 0.7 copy-start.9
  114.7 3.4 copy-start.8
  116.6 0.6 copy-start.20
  118.1 3.5 copy-start.21
  121.6 0.6 copy-start.26
  145.6 4.3 copy-start.15
  145.6 4.3 copy-start.27
  145.6 4.3 copy-start.29
  145.6 5.3 copy-start.7
  150.1 0.7 copy-start.5
  153.8 4.6 copy-start.10
  157.3 1.1 copy-start
  162.0 49.0 %reduce-scatter.21.cloned.1.call-start = ((), (), s32[]{:S(2)}) async-start(), calls=%async_computation.16 | async-start | bytes 983040
  164.9 5.2 copy-start.12
  164.9 5.2 copy-start.16
  167.3 4.7 copy-start.19
  167.3 4.7 copy-start.28
  167.3 4.7 copy-start.30
  167.3 71.9 %reduce-scatter.13.cloned.1.call-start = ((), (), s32[]{:S(2)}) async-start(), calls=%async_computation.12 | async-start | bytes 1474560 | tf_op jit(solution)/shard_map/reduce_scatter | solution.py:203
  170.0 101.6 %reduce-scatter.17.cloned.1.call-start = ((), (), s32[]{:S(2)}) async-start(), calls=%async_computation.14 | async-start | bytes 2211840 | tf_op jit(solution)/shard_map/reduce_scatter | solution.py:212
  171.9 4.3 copy-start.1
  172.0 4.3 copy-start.4
  172.0 142.6 %reduce-scatter.15.cloned.1.call-start = ((), (), s32[]{:S(2)}) async-start(), calls=%async_computation.13 | async-start | bytes 4423680 | tf_op jit(solution)/shard_map/reduce_scatter | solution.py:209
  176.2 10.4 %copy-start.14 = (f32[128,64]{0,1:T(8,128)S(1)}, f32[128,64]{0,1:T(8,128)}, u32[]{:S(2)}) copy-start(f32[128,64]{0,1:T(8,128)} %copy-done.13) | copy-start | bytes 98308
  176.2 10.4 %copy-start.18 = (f32[128,64]{0,1:T(8,128)S(1)}, f32[128,64]{0,1:T(8,128)}, u32[]{:S(2)}) copy-start(f32[128,64]{0,1:T(8,128)} %copy-done.17) | copy-start | bytes 98308
  176.2 181.1 %reduce-scatter.11.cloned.1.call-start = ((), (), s32[]{:S(2)}) async-start(), calls=%async_computation.11 | async-start | bytes 4423680 | tf_op jit(solution)/shard_map/reduce_scatter | solution.py:200
  176.9 35.2 %copy-start.3 = (bf16[1,128,768]{2,1,0:T(8,128)(2,1)S(1)}, bf16[1,128,768]{2,1,0:T(8,128)(2,1)}, u32[]{:S(2)}) copy-start(bf16[1,128,768]{2,1,0:T(8,128)(2,1)} %param.8) | copy-start | bytes 589828
  176.9 35.2 %copy-start.23 = (f32[128]{0:T(128)S(1)}, f32[128]{0:T(128)}, u32[]{:S(2)}) copy-start(f32[128]{0:T(128)} %copy-done.22) | copy-start | bytes 1540
  176.9 35.2 %copy-start.25 = (f32[128]{0:T(128)S(1)}, f32[128]{0:T(128)}, u32[]{:S(2)}) copy-start(f32[128]{0:T(128)} %copy-done.24) | copy-start | bytes 1540
  215.2 1.5 copy-start.11
  217.8 3.7 copy-start.32
  217.8 9.6 %copy-start.6 = (f32[128,768]{1,0:T(8,128)S(1)}, f32[128,768]{1,0:T(8,128)}, u32[]{:S(2)}) copy-start(f32[128,768]{1,0:T(8,128)} %copy-done.5) | copy-start | bytes 1179652
Sparse Core Ops, SparseCore 0:
  9.5 52.5 all-gather.4
  63.6 22.5 all-gather.6
  87.8 25.9 all-gather.8
  115.2 30.3 all-gather.10
  162.2 23.1 reduce-scatter.18
  187.8 23.1 reduce-scatter.20
  213.6 25.6 reduce-scatter.12
  242.4 29.1 reduce-scatter.16
  274.1 40.3 reduce-scatter.14
  316.9 40.3 reduce-scatter.10
